TPU v7x, 256 devices: a whole 4x4x8 slice. The times are simulated.
256 devices in a mesh: pw: 64 (over x_lo, z, y), band: 4 (over x_hi, core).
Axes of the slice: x: 4 (x_hi: 2, x_lo: 2; x = x_hi * 2 + x_lo), y: 4, z: 8, core: 2. Of those that a mesh axis runs over, the one named last changes fastest.
Arguments:
- residual_directions: float32 [2, 512, 4, 16384], P(None, 'pw', 'band'), may hold values from -6 to 6
- local_field_applied: float32 [2, 512, 4, 16384], P(None, 'pw', 'band'), may hold values from -6 to 6
- orbital_running_sum: bfloat16 [2, 2048, 4, 16384], P(None, None, 'band', 'pw'), may hold values from -6 to 6
- energy_operator_running_sum: bfloat16 [2, 2048, 4, 16384], P(None, None, 'band', 'pw'), may hold values from -6 to 6
- coefficient_store: bfloat16 [4, 512, 2048], P('band'), may hold values from -0.25 to 0.25
- slab_keepers: int32 [2], replicated, may hold values from 0 to 3
- lattice_position: int32 [4, 16384], P('band', 'pw'), may hold values from 0 to 262143
Outputs:
- psi_new: bfloat16 [2, 2048, 4, 16384], P(None, None, 'band', 'pw')
- hpsi_new: bfloat16 [2, 2048, 4, 16384], P(None, None, 'band', 'pw')
Inputs may be any that keep to these rules, and one draw needn't show every extreme that they name: `slab_keepers`: each panel's owner is an index along band. `lattice_position`: grid points are row-major indices of a 64 x 64 x 64 grid, not necessarily distinct.
All inputs are finite; a program needn't handle non-finite values.
Results may differ from a plain program's by a relative error of at most 0.001.
Values may be sent and summed in bfloat16 or wider, within the bound.
No kernel may reach another device: no remote copies, remote signals or barrier semaphores. Data moves between devices by JAX's collectives and lax.ppermute only.
A program may use at most 128 MiB of HBM per device.

v0:
```python
import jax
import jax.numpy as jnp
from jax import lax
from jax.sharding import PartitionSpec as P

RESIDUAL_NUMBER = 512
SLAB_LENGTH = 256
GRID = 64


def from_root(value, axis, source):
    kept = jnp.where(lax.axis_index(axis) == source, value, 0).astype(value.dtype)
    return lax.psum(kept, axis)


def kinetic_of(lattice_position):
    first = lattice_position // (GRID * GRID)
    second = lattice_position // GRID % GRID
    third = lattice_position % GRID
    total = jnp.zeros(lattice_position.shape, jnp.int32)
    for index in (first, second, third):
        folded = jnp.where(index >= GRID // 2, index - GRID, index)
        total = total + folded * folded
    return total.astype(jnp.float32) / (GRID * GRID)


def rotate_plane(panels, plane):
    total = None
    for subspace_slab in range(len(panels)):
        block = plane[subspace_slab * SLAB_LENGTH : (subspace_slab + 1) * SLAB_LENGTH]
        term = lax.dot_general(
            panels[subspace_slab],
            block,
            (((0,), (0,)), ((), ())),
            precision=lax.Precision.HIGHEST,
            preferred_element_type=jnp.float32,
        )
        total = term if total is None else total + term
    return total


def per_device(
    residual_directions,
    local_field_applied,
    orbital_running_sum,
    energy_operator_running_sum,
    coefficient_store,
    slab_keepers,
    lattice_position,
):
    count = RESIDUAL_NUMBER // SLAB_LENGTH
    panels = []
    for subspace_slab in range(count):
        slab_piece = coefficient_store[
            0, subspace_slab * SLAB_LENGTH : (subspace_slab + 1) * SLAB_LENGTH
        ]
        panels.append(
            from_root(slab_piece, "band", slab_keepers[subspace_slab]).astype(jnp.float32)
        )
    outgoing = (residual_directions, local_field_applied)
    local_kinetic = kinetic_of(lattice_position)
    corr_part = lax.all_to_all(outgoing[0], "pw", split_axis=3, concat_axis=1, tiled=True)
    second_part = lax.all_to_all(outgoing[1], "pw", split_axis=3, concat_axis=1, tiled=True)
    planes_count = corr_part.shape[0]
    rows = corr_part.shape[1]
    width = corr_part.shape[3]
    corr_flat = corr_part.reshape(planes_count, rows, width)
    second_flat = second_part.reshape(planes_count, rows, width)
    hcorr_flat = local_kinetic.reshape(1, 1, width) * corr_flat + second_flat
    psi_planes = [
        rotate_plane(panels, corr_flat[plane_index]) for plane_index in range(planes_count)
    ]
    hpsi_planes = [
        rotate_plane(panels, hcorr_flat[plane_index]) for plane_index in range(planes_count)
    ]
    span = psi_planes[0].shape[0]
    psi_stack = jnp.stack(psi_planes, axis=0).reshape(planes_count, span, 1, width)
    hpsi_stack = jnp.stack(hpsi_planes, axis=0).reshape(planes_count, span, 1, width)
    psi_new = (orbital_running_sum.astype(jnp.float32) + psi_stack).astype(jnp.bfloat16)
    hpsi_new = (energy_operator_running_sum.astype(jnp.float32) + hpsi_stack).astype(jnp.bfloat16)
    return (psi_new, hpsi_new)


def solution(mesh):
    in_specs = (
        P(None, "pw", "band", None),
        P(None, "pw", "band", None),
        P(None, None, "band", "pw"),
        P(None, None, "band", "pw"),
        P("band", None, None),
        P(),
        P("band", "pw"),
    )
    out_specs = (P(None, None, "band", "pw"), P(None, None, "band", "pw"))
    return jax.shard_map(
        per_device, mesh=mesh, in_specs=in_specs, out_specs=out_specs, check_vma=False
    )
```

profile of v0, /device:TPU:6, one launch (start us, length us, event | category | flops | bytes accessed | tf_op | source)
XLA Modules:
  0.0 261.7 jit_solution(14496637142903261948)
XLA Ops:
  7.2 17.4 %copy.42 = f32[2,8,1,16384]{1,0,2,3:T(2,128)} copy(f32[2,8,1,16384]{3,2,1,0:T(1,128)} %param.7) | data formatting | bytes 2097152 | tf_op args[0]
  24.6 29.0 %reshape.42 = f32[64,1,4096]{2,1,0:T(1,128)} reshape(f32[16384,1,2,8]{3,2,1,0:T(2,128)} %bitcast.92) | data formatting | bytes 2097152
  53.5 0.0 copy-start.4
  53.5 13.3 %all-to-all-start = ((f32[64,1,4096]{2,1,0:T(1,128)}), f32[64,1,4096]{2,1,0:T(1,128)S(1)}, u32[]{:S(2)}, u32[]{:S(2)}) async-start(f32[64,1,4096]{2,1,0:T(1,128)} %reshape.42), calls=%async_computation | async-start | bytes 2097152 | tf_op jit(solution)/shard_map/all_to_all | solution.py:62
  66.9 0.0 copy-done.4
  66.9 14.6 %copy.50 = f32[2,8,1,16384]{1,0,2,3:T(2,128)} copy(f32[2,8,1,16384]{3,2,1,0:T(1,128)S(1)} %copy-done.4) | data formatting | bytes 2097152 | tf_op args[1]
  81.4 28.9 %reshape.44 = f32[64,1,4096]{2,1,0:T(1,128)} reshape(f32[16384,1,2,8]{3,2,1,0:T(2,128)} %bitcast.93) | data formatting | bytes 2097152
  110.4 0.0 copy-start.8
  110.4 0.0 all-to-all-done
  110.4 11.6 %all-to-all-start.1 = ((f32[64,1,4096]{2,1,0:T(1,128)}), f32[64,1,4096]{2,1,0:T(1,128)}, u32[]{:S(2)}, u32[]{:S(2)}) async-start(f32[64,1,4096]{2,1,0:T(1,128)} %reshape.44), calls=%async_computation.1 | async-start | bytes 2097152 | tf_op jit(solution)/shard_map/all_to_all | solution.py:63
  122.0 0.2 all-reduce.3.cloned.1.call-start
  122.2 0.0 copy-done.8
  122.3 0.6 fusion.29
  124.1 3.0 %select_bitcast_fusion = (bf16[256,2048]{1,0:T(8,128)(2,1)}, bf16[256,2048]{1,0:T(8,128)(2,1)}) fusion(bf16[1,512,2048]{2,1,0:T(8,128)(2,1)} %param.11, pred[]{:T(512)S(6)} %eq.10, pred[]{:T(512)S(6)} %eq.9), kind=kLoop, calls=%fused_computation.18 | loop fusion | flops 1048576 | bytes 4194306 | tf_op jit(solution)/shard_map/jit(_where)/select_n | solution.py:12
  127.1 0.0 copy-start.9
  127.1 0.0 all-reduce.3.cloned.1.call-update
  127.2 0.7 copy-done.9
  127.8 0.6 broadcast.42
  128.4 3.3 %reduce.1 = f32[64,4096]{1,0:T(8,128)S(1)} reduce(f32[64,1,4096]{2,1,0:T(1,128)S(1)} %all-to-all-done, f32[]{:T(128)} %broadcast.42), dimensions={1}, to_apply=%all_to_all.22.reduce_sub_computation | reduce | bytes 2097156 | tf_op jit(solution)/shard_map/all_to_all | solution.py:62
  131.7 26.7 %reshape.43 = f32[16384,1,2,8]{3,2,1,0:T(2,128)} reshape(f32[64,4096]{1,0:T(8,128)S(1)} %reduce.1) | data formatting | bytes 2097152
  158.4 17.8 %copy.56 = f32[2,8,1,64,256]{4,1,3,0,2:T(8,128)S(1)} copy(f32[2,8,1,64,256]{1,0,4,3,2:T(2,128)} %bitcast.89) | data formatting | bytes 2097152 | tf_op jit(solution)/shard_map/all_to_all | solution.py:62
  176.2 13.2 %copy.55 = f32[2,8,1,64,256]{4,3,1,0,2:T(8,128)S(1)} copy(f32[2,8,1,64,256]{1,0,4,3,2:T(2,128)} %bitcast.90) | data formatting | bytes 2097152 | tf_op jit(solution)/shard_map/all_to_all | solution.py:62
  189.4 0.0 all-to-all-done.1
  189.4 4.4 %reduce = f32[64,4096]{1,0:T(8,128)S(1)} reduce(f32[64,1,4096]{2,1,0:T(1,128)} %all-to-all-done.1, f32[]{:T(128)} %broadcast.42), dimensions={1}, to_apply=%all_to_all.25.reduce_sub_computation | reduce | bytes 2097156 | tf_op jit(solution)/shard_map/all_to_all | solution.py:63
  193.8 26.7 %reshape.45 = f32[16384,1,2,8]{3,2,1,0:T(2,128)} reshape(f32[64,4096]{1,0:T(8,128)S(1)} %reduce) | data formatting | bytes 2097152
  220.5 17.8 %copy.58 = f32[2,8,1,64,256]{4,1,3,0,2:T(8,128)S(1)} copy(f32[2,8,1,64,256]{1,0,4,3,2:T(2,128)} %bitcast.91) | data formatting | bytes 2097152 | tf_op jit(solution)/shard_map/all_to_all | solution.py:63
  238.4 0.9 fusion.28
  239.3 0.1 bitcast_add_fusion
  239.4 0.0 all-reduce.3.cloned.1.call-done
  239.4 0.0 copy-start
  239.4 2.6 fusion.10
  242.0 0.0 copy-done
  242.0 0.0 copy-start.1
  242.0 1.3 fusion.11
  243.3 0.0 copy-done.1
  243.3 1.3 fusion.4
  244.6 0.0 copy-start.5
  244.6 1.3 fusion.5
  246.0 0.0 copy-done.5
  246.0 1.3 fusion.13
  247.3 0.0 copy-start.7
  247.3 1.3 fusion.16
  248.7 0.0 copy-done.7
  248.7 0.0 copy-start.6
  248.7 1.4 fusion.6
  250.1 0.0 copy-done.6
  250.1 0.0 copy-start.2
  250.1 0.0 copy-start.3
  250.1 1.4 fusion.7
  251.5 0.2 copy-done.2
  251.7 0.6 copy-done.3
  252.3 2.5 fusion.8
  (1 shorter events, 0.0 us)
Async XLA Ops:
  53.5 13.4 %copy-start.4 = (f32[2,8,1,16384]{3,2,1,0:T(1,128)S(1)}, f32[2,8,1,16384]{3,2,1,0:T(1,128)}, u32[]{:S(2)}) copy-start(f32[2,8,1,16384]{3,2,1,0:T(1,128)} %param.8) | copy-start | bytes 3145732
  53.5 56.9 %all-to-all-start = ((f32[64,1,4096]{2,1,0:T(1,128)}), f32[64,1,4096]{2,1,0:T(1,128)S(1)}, u32[]{:S(2)}, u32[]{:S(2)}) async-start(f32[64,1,4096]{2,1,0:T(1,128)} %reshape.42), calls=%async_computation | async-start | bytes 2097152 | tf_op jit(solution)/shard_map/all_to_all | solution.py:62
  110.4 11.9 %copy-start.8 = (s32[2]{0:T(128)S(1)}, s32[2]{0:T(128)}, u32[]{:S(2)}) copy-start(s32[2]{0:T(128)} %param.12) | copy-start | bytes 28
  110.4 79.0 %all-to-all-start.1 = ((f32[64,1,4096]{2,1,0:T(1,128)}), f32[64,1,4096]{2,1,0:T(1,128)}, u32[]{:S(2)}, u32[]{:S(2)}) async-start(f32[64,1,4096]{2,1,0:T(1,128)} %reshape.44), calls=%async_computation.1 | async-start | bytes 2097152 | tf_op jit(solution)/shard_map/all_to_all | solution.py:63
  122.0 117.4 %all-reduce.3.cloned.1.call-start = ((), (), s32[]{:S(2)}) async-start(), calls=%async_computation.2 | async-start | bytes 4194304 | tf_op jit(solution)/shard_map/psum | solution.py:13
  127.1 0.7 copy-start.9
  239.4 2.6 copy-start
  242.0 1.3 copy-start.1
  244.6 1.3 copy-start.5
  247.3 1.4 copy-start.7
  248.7 1.4 copy-start.6
  250.1 1.6 copy-start.2
  250.1 2.2 copy-start.3
Sparse Core Ops, SparseCore 0:
  127.3 65.1 all-reduce.2
where the time goes:
time: 265 us; the launch traced here: 262 us
  local copies, waits for them, and re-layouts  196 us (74%)
  starting transfers between devices  25.2 us (10%)
  between operations  15.6 us (6%)
  other arithmetic  13.3 us (5%)
  matrix products  11.9 us (4%)
    unnamed x26, local copies, waits for them, and re-layouts  145 us
    all_to_all x2, local copies, waits for them, and re-layouts, per_device(): lax.all_to_all(outgoing[0], 'pw', split_axis=3, concat_axis=1, tiled=True)  31 us
    all_to_all x2, local copies, waits for them, and re-layouts, per_device(): lax.all_to_all(outgoing[1], 'pw', split_axis=3, concat_axis=1, tiled=True)  18.4 us
    all_to_all x1, starting transfers between devices, per_device(): lax.all_to_all(outgoing[0], 'pw', split_axis=3, concat_axis=1, tiled=True)  13.3 us
    dot_general x8, matrix products, rotate_plane(): lax.dot_general(panels[subspace_slab], block, (((0,), (0,)), ((), ())), p...  11.9 us
    all_to_all x1, starting transfers between devices, per_device(): lax.all_to_all(outgoing[1], 'pw', split_axis=3, concat_axis=1, tiled=True)  11.6 us
  transfers between devices with their start and end apart: 3, of which 0 were waited for; matrix products, arithmetic and copies ran while one was open for 61% of the time, Pallas kernels for 0%

commit v1 on v0

--- a/solution.py
+++ b/solution.py
@@ -59,7 +59,10 @@
         )
     outgoing = (residual_directions, local_field_applied)
     local_kinetic = kinetic_of(lattice_position)
-    corr_part = lax.all_to_all(outgoing[0], "pw", split_axis=3, concat_axis=1, tiled=True)
+    corr_part = jnp.concatenate(
+        lax.all_to_all(jnp.stack(jnp.split(outgoing[0], lax.axis_size("pw"), axis=3)), "pw", 0, 0),
+        axis=1,
+    )
     second_part = lax.all_to_all(outgoing[1], "pw", split_axis=3, concat_axis=1, tiled=True)
     planes_count = corr_part.shape[0]
     rows = corr_part.shape[1]

time: 265 us -> 216 us (0.82)
  the two profiles are of different devices: /device:TPU:6 before, /device:TPU:1 now
where the time goes in v1:
time: 216 us; the launch traced here: 214 us
  local copies, waits for them, and re-layouts  133 us (62%)
  starting transfers between devices  24.5 us (11%)
  waiting for transfers between devices  19.5 us (9%)
  between operations  15.6 us (7%)
  matrix products  11.7 us (5%)
  other arithmetic  9.92 us (5%)
    unnamed x82, local copies, waits for them, and re-layouts  112 us
    psum x1, waiting for transfers between devices, from_root(): return lax.psum(kept, axis)  19.4 us
    all_to_all x2, local copies, waits for them, and re-layouts, per_device(): lax.all_to_all(outgoing[1], 'pw', split_axis=3, concat_axis=1, tiled=True)  18.4 us
    all_to_all x1, starting transfers between devices, per_device(): lax.all_to_all(outgoing[1], 'pw', split_axis=3, concat_axis=1, tiled=True)  13.7 us
    dot_general x8, matrix products, rotate_plane(): lax.dot_general(panels[subspace_slab], block, (((0,), (0,)), ((), ())), p...  11.7 us
    all_to_all x1, starting transfers between devices, per_device(): lax.all_to_all(jnp.stack(jnp.split(outgoing[0], lax.axis_size('pw'), axis...  10.7 us
  transfers between devices with their start and end apart: 3, of which 1 were waited for; matrix products, arithmetic and copies ran while one was open for 43% of the time, Pallas kernels for 0%

profile of v1, /device:TPU:1, one launch (start us, length us, event | category | flops | bytes accessed | tf_op | source)
XLA Modules:
  0.0 214.1 jit_solution(15320392186818600661)
XLA Ops:
  7.2 17.4 %copy.289 = f32[2,8,1,16384]{1,0,2,3:T(2,128)} copy(f32[2,8,1,16384]{3,2,1,0:T(1,128)} %param.8) | data formatting | bytes 2097152 | tf_op args[1]
  24.5 29.0 %reshape.41 = f32[64,1,4096]{2,1,0:T(1,128)} reshape(f32[16384,1,2,8]{3,2,1,0:T(2,128)} %bitcast.344) | data formatting | bytes 2097152
  53.5 13.7 %all-to-all-start.1 = ((f32[64,1,4096]{2,1,0:T(1,128)}), f32[64,1,4096]{2,1,0:T(1,128)S(1)}, u32[]{:S(2)}, u32[]{:S(2)}) async-start(f32[64,1,4096]{2,1,0:T(1,128)} %reshape.41), calls=%async_computation.1 | async-start | bytes 2097152 | tf_op jit(solution)/shard_map/all_to_all | solution.py:66
  68.2 0.6 constant_dynamic-update-slice_fusion.63
  69.4 0.6 constant_dynamic-update-slice_fusion.61
  70.0 0.6 constant_dynamic-update-slice_fusion.60
  70.6 0.6 constant_dynamic-update-slice_fusion.59
  71.2 0.6 constant_dynamic-update-slice_fusion.58
  71.8 0.6 constant_dynamic-update-slice_fusion.57
  72.4 0.6 constant_dynamic-update-slice_fusion.56
  73.0 0.6 constant_dynamic-update-slice_fusion.55
  73.6 0.6 constant_dynamic-update-slice_fusion.54
  74.8 0.6 constant_dynamic-update-slice_fusion.52
  75.4 0.6 constant_dynamic-update-slice_fusion.51
  76.6 0.6 constant_dynamic-update-slice_fusion.49
  77.2 0.6 constant_dynamic-update-slice_fusion.48
  78.4 0.6 constant_dynamic-update-slice_fusion.46
  79.0 0.6 constant_dynamic-update-slice_fusion.45
  79.6 0.6 constant_dynamic-update-slice_fusion.44
  80.2 0.6 constant_dynamic-update-slice_fusion.43
  80.8 0.6 constant_dynamic-update-slice_fusion.42
  82.0 0.6 constant_dynamic-update-slice_fusion.40
  83.2 0.6 constant_dynamic-update-slice_fusion.38
  84.4 0.6 constant_dynamic-update-slice_fusion.36
  85.0 0.6 constant_dynamic-update-slice_fusion.35
  86.2 0.6 constant_dynamic-update-slice_fusion.33
  86.8 0.6 constant_dynamic-update-slice_fusion.32
  88.0 0.6 constant_dynamic-update-slice_fusion.30
  88.6 0.6 constant_dynamic-update-slice_fusion.29
  89.2 0.6 constant_dynamic-update-slice_fusion.28
  91.0 0.6 constant_dynamic-update-slice_fusion.25
  91.6 0.6 constant_dynamic-update-slice_fusion.24
  92.2 0.6 constant_dynamic-update-slice_fusion.23
  92.8 0.6 constant_dynamic-update-slice_fusion.22
  94.6 0.6 constant_dynamic-update-slice_fusion.19
  95.2 0.6 constant_dynamic-update-slice_fusion.18
  96.4 0.6 constant_dynamic-update-slice_fusion.16
  97.0 0.6 constant_dynamic-update-slice_fusion.15
  97.6 0.6 constant_dynamic-update-slice_fusion.14
  100.6 0.6 constant_dynamic-update-slice_fusion.9
  103.1 0.6 constant_dynamic-update-slice_fusion.8
  103.8 0.6 constant_dynamic-update-slice_fusion.7
  105.6 0.6 constant_dynamic-update-slice_fusion.4
  106.2 0.6 constant_dynamic-update-slice_fusion.3
  106.8 0.6 constant_dynamic-update-slice_fusion.2
  108.0 0.6 constant_dynamic-update-slice_fusion
  108.6 10.7 %all-to-all-start = ((f32[64,2,8,1,256]{4,2,1,3,0:T(8,128)}), f32[64,2,8,1,256]{4,2,1,3,0:T(8,128)S(1)}, u32[]{:S(2)}, u32[]{:S(2)}) async-start(f32[64,2,8,1,256]{4,2,1,3,0:T(8,128)} %constant_dynamic-update-slice_fusion), calls=%async_computation | async-start | bytes 2097152 | tf_op jit(solution)/shard_map/all_to_all | solution.py:63
  119.3 3.0 %select_bitcast_fusion = (bf16[256,2048]{1,0:T(8,128)(2,1)}, bf16[256,2048]{1,0:T(8,128)(2,1)}) fusion(bf16[1,512,2048]{2,1,0:T(8,128)(2,1)} %param.11, pred[]{:T(512)S(6)} %eq.10, pred[]{:T(512)S(6)} %eq.9), kind=kLoop, calls=%fused_computation.18 | loop fusion | flops 1048576 | bytes 4194306 | tf_op jit(solution)/shard_map/jit(_where)/select_n | solution.py:12
  122.4 0.7 copy-done.7
  123.6 3.3 %reduce = f32[64,4096]{1,0:T(8,128)S(1)} reduce(f32[64,1,4096]{2,1,0:T(1,128)S(1)} %all-to-all-done.1, f32[]{:T(128)} %broadcast.42), dimensions={1}, to_apply=%all_to_all.15.reduce_sub_computation | reduce | bytes 2097156 | tf_op jit(solution)/shard_map/all_to_all | solution.py:66
  127.0 26.7 %reshape.42 = f32[16384,1,2,8]{3,2,1,0:T(2,128)} reshape(f32[64,4096]{1,0:T(8,128)S(1)} %reduce) | data formatting | bytes 2097152
  153.6 17.8 %copy.295 = f32[2,8,1,64,256]{4,1,3,0,2:T(8,128)S(1)} copy(f32[2,8,1,64,256]{1,0,4,3,2:T(2,128)} %bitcast.343) | data formatting | bytes 2097152 | tf_op jit(solution)/shard_map/all_to_all | solution.py:66
  171.5 1.1 bitcast_add_fusion
  172.7 19.4 %all-reduce.3.cloned.1.call-done = (bf16[256,2048]{1,0:T(8,128)(2,1)}, bf16[256,2048]{1,0:T(8,128)(2,1)}) async-done(((bf16[256,2048]{1,0:T(8,128)(2,1)}, bf16[256,2048]{1,0:T(8,128)(2,1)}), (bf16[256,2048]{1,0:T(8,128)(2,1)}, bf16[256,2048]{1,0:T(8,128)(2,1)})) %all-reduce.3.cloned.1.call-update) | async-done | bytes 2097168 | tf_op jit(solution)/shard_map/psum | solution.py:13
  192.1 2.6 %fusion.10 = f32[2048,256]{1,0:T(8,128)S(1)} fusion(bf16[256,2048]{1,0:T(8,128)(2,1)} %get-tuple-element.12, f32[2,512,256]{2,1,0:T(8,128)} %bitcast_add_fusion), kind=kOutput, calls=%fused_computation.23 | convolution fusion | flops 1610612736 | bytes 3407872 | tf_op jit(solution)/shard_map/dot_general | solution.py:31
  194.7 1.3 fusion.11
  196.0 1.3 fusion.12
  197.3 1.3 fusion.13
  198.5 1.3 fusion.4
  199.9 1.3 fusion.5
  201.2 1.3 fusion.6
  202.6 1.3 fusion.7
  204.1 0.6 copy-done.4
  204.8 2.5 %fusion.8 = (bf16[2,2048,1,256]{3,1,2,0:T(8,128)(2,1)}, bf16[2,2048,1,256]{3,1,2,0:T(8,128)(2,1)}) fusion(f32[1,2048,256]{2,1,0:T(8,128)S(1)} %fusion.4, f32[1,2048,256]{2,1,0:T(8,128)S(1)} %fusion.5, bf16[2,2048,1,256]{3,1,2,0:T(8,128)(2,1)S(1)} %copy-done.3, f32[1,2048,256]{2,1,0:T(8,128)S(1)} %fusion.6, f32[1,2048,256]{2,1,0:T(8,128)S(1)} %fusion.7, ...), kind=kLoop, calls=%fused_computation.14 | loop fusion | flops 8388608 | bytes 16777216
  (47 shorter events, 15.1 us)
Async XLA Ops:
  53.5 13.7 %copy-start.5 = (f32[2,8,1,16384]{3,2,1,0:T(1,128)S(1)}, f32[2,8,1,16384]{3,2,1,0:T(1,128)}, u32[]{:S(2)}) copy-start(f32[2,8,1,16384]{3,2,1,0:T(1,128)} %param.7) | copy-start | bytes 3145732
  53.5 55.1 %all-to-all-start.1 = ((f32[64,1,4096]{2,1,0:T(1,128)}), f32[64,1,4096]{2,1,0:T(1,128)S(1)}, u32[]{:S(2)}, u32[]{:S(2)}) async-start(f32[64,1,4096]{2,1,0:T(1,128)} %reshape.41), calls=%async_computation.1 | async-start | bytes 2097152 | tf_op jit(solution)/shard_map/all_to_all | solution.py:66
  67.2 34.0 %copy-start.6 = (s32[2]{0:T(128)S(1)}, s32[2]{0:T(128)}, u32[]{:S(2)}) copy-start(s32[2]{0:T(128)} %param.12) | copy-start | bytes 28
  108.6 62.9 %all-to-all-start = ((f32[64,2,8,1,256]{4,2,1,3,0:T(8,128)}), f32[64,2,8,1,256]{4,2,1,3,0:T(8,128)S(1)}, u32[]{:S(2)}, u32[]{:S(2)}) async-start(f32[64,2,8,1,256]{4,2,1,3,0:T(8,128)} %constant_dynamic-update-slice_fusion), calls=%async_computation | async-start | bytes 2097152 | tf_op jit(solution)/shard_map/all_to_all | solution.py:63
  119.3 72.8 %all-reduce.3.cloned.1.call-start = ((), (), s32[]{:S(2)}) async-start(), calls=%async_computation.2 | async-start | bytes 4194304 | tf_op jit(solution)/shard_map/psum | solution.py:13
  122.3 0.7 copy-start.7
  172.7 22.1 %copy-start.2 = (f32[2,512,256]{2,1,0:T(8,128)S(1)}, f32[2,512,256]{2,1,0:T(8,128)}, u32[]{:S(2)}) copy-start(f32[2,512,256]{2,1,0:T(8,128)} %bitcast_add_fusion) | copy-start | bytes 3145732
  192.1 2.6 %copy-start = (bf16[256,2048]{1,0:T(8,128)(2,1)S(1)}, bf16[256,2048]{1,0:T(8,128)(2,1)}, u32[]{:S(2)}) copy-start(bf16[256,2048]{1,0:T(8,128)(2,1)} %get-tuple-element.12) | copy-start | bytes 3145732
  197.3 1.3 copy-start.1
  202.5 1.6 copy-start.3
  202.5 2.2 %copy-start.4 = (bf16[2,2048,1,256]{3,1,2,0:T(8,128)(2,1)S(1)}, bf16[2,2048,1,256]{3,1,2,0:T(8,128)(2,1)}, u32[]{:S(2)}) copy-start(bf16[2,2048,1,256]{3,1,2,0:T(8,128)(2,1)} %param.9) | copy-start | bytes 6291460
Sparse Core Ops, SparseCore 0:
  123.4 68.6 all-reduce.2
